TPU v7x, 256 devices: a whole 4x4x8 slice. The times are simulated.
256 devices in a mesh: row: 16 (over z, core), col: 16 (over y, x).
Axes of the slice: x: 4, y: 4, z: 8, core: 2. Of those that a mesh axis runs over, the one named last changes fastest.
Arguments:
- inputs: bfloat16 [512, 16384], P('col', 'row'), may hold values from -6 to 6
- output_gradient: bfloat16 [512, 16384], P('col', 'row'), may hold values from -6 to 6
- gate_matrix: bfloat16 [16384, 26624], P('row', 'col'), may hold values from -0.046875 to 0.046875
- up_matrix: bfloat16 [16384, 26624], P('row', 'col'), may hold values from -0.046875 to 0.046875
- down_matrix: bfloat16 [26624, 16384], P('col', 'row'), may hold values from -0.046875 to 0.046875
- gate_adapter_first: bfloat16 [16384, 512], P('row', 'col'), may hold values from -0.046875 to 0.046875
- gate_adapter_second: bfloat16 [512, 26624], P('row', 'col'), may hold values from -0.25 to 0.25
- up_adapter_first: bfloat16 [16384, 512], P('row', 'col'), may hold values from -0.046875 to 0.046875
- up_adapter_second: bfloat16 [512, 26624], P('row', 'col'), may hold values from -0.25 to 0.25
- down_adapter_first: bfloat16 [26624, 512], P('col', 'row'), may hold values from -0.25 to 0.25
- down_adapter_second: bfloat16 [512, 16384], P('col', 'row'), may hold values from -0.046875 to 0.046875
Outputs:
- input_grad: bfloat16 [512, 16384], P('col', 'row')
- grad_gate_in: float32 [16384, 512], P('row', 'col')
- grad_gate_out: float32 [512, 26624], P('row', 'col')
- grad_up_in: float32 [16384, 512], P('row', 'col')
- grad_up_out: float32 [512, 26624], P('row', 'col')
- grad_down_in: float32 [26624, 512], P('col', 'row')
- grad_down_out: float32 [512, 16384], P('col', 'row')
All inputs are finite; a program needn't handle non-finite values.
Results may differ from a plain program's by a relative error of at most 0.0062.
Values may be sent and summed in bfloat16 or wider, within the bound.
No kernel may reach another device: no remote copies, remote signals or barrier semaphores. Data moves between devices by JAX's collectives and lax.ppermute only.
A program may use at most 128 MiB of HBM per device.

v0:
```python
import jax
import jax.numpy as jnp
from jax import lax
from jax.sharding import PartitionSpec as P


def matrix_product(first_mat, second_mat):
    return jnp.dot(first_mat, second_mat, preferred_element_type=jnp.float32)


def product_transposed(first_mat, second_mat):
    return lax.dot_general(
        first_mat, second_mat, (((1,), (1,)), ((), ())), preferred_element_type=jnp.float32
    )


def product_tn(first_mat, second_mat):
    return lax.dot_general(
        first_mat, second_mat, (((0,), (0,)), ((), ())), preferred_element_type=jnp.float32
    )


def gated_back(gate_pre, up_pre, hid_grad):
    sigmoid_g = jax.nn.sigmoid(gate_pre)
    silu_g = gate_pre * sigmoid_g
    hidden_state = (silu_g * up_pre).astype(jnp.bfloat16)
    gate_gradient = (hid_grad * up_pre * sigmoid_g * (1.0 + gate_pre * (1.0 - sigmoid_g))).astype(
        jnp.bfloat16
    )
    up_gradient = (hid_grad * silu_g).astype(jnp.bfloat16)
    return (hidden_state, gate_gradient, up_gradient)


def on_device(
    inputs,
    output_gradient,
    gate_matrix,
    up_matrix,
    down_matrix,
    gate_adapter_first,
    gate_adapter_second,
    up_adapter_first,
    up_adapter_second,
    down_adapter_first,
    down_adapter_second,
):
    row_index = lax.axis_index("row")
    col_index = lax.axis_index("col")
    input_row_block, cotangent_rows = (
        lax.all_gather(inputs, "col", axis=0, tiled=True),
        lax.all_gather(output_gradient, "col", axis=0, tiled=True),
    )
    rank_column = gate_adapter_first.shape[1]
    rank_row_index = gate_adapter_second.shape[0]
    portion_gate = matrix_product(input_row_block, gate_adapter_first)
    portion_up = matrix_product(input_row_block, up_adapter_first)
    portion_down = product_transposed(cotangent_rows, down_adapter_second)
    sum_gate, sum_up, sum_down = lax.psum((portion_gate, portion_up, portion_down), "row")
    reduced_gate, reduced_up, reduced_cotangent = (
        lax.all_gather(sum_gate.astype(jnp.bfloat16), "col", axis=1, tiled=True),
        lax.all_gather(sum_up.astype(jnp.bfloat16), "col", axis=1, tiled=True),
        lax.all_gather(sum_down.astype(jnp.bfloat16), "col", axis=1, tiled=True),
    )
    row_start = row_index * rank_row_index
    reduced_gate_row = lax.dynamic_slice_in_dim(reduced_gate, row_start, rank_row_index, 1)
    reduced_up_row = lax.dynamic_slice_in_dim(reduced_up, row_start, rank_row_index, 1)
    reduced_cotangent_row = lax.dynamic_slice_in_dim(
        reduced_cotangent, row_start, rank_row_index, 1
    )
    gate_portion = matrix_product(input_row_block, gate_matrix) + matrix_product(
        reduced_gate_row, gate_adapter_second
    )
    up_portion = matrix_product(input_row_block, up_matrix) + matrix_product(
        reduced_up_row, up_adapter_second
    )
    hidden_portion = product_transposed(cotangent_rows, down_matrix) + product_transposed(
        reduced_cotangent_row, down_adapter_first
    )
    gate_pre, up_pre, hid_grad = (
        lax.psum_scatter(gate_portion, "row", scatter_dimension=0, tiled=True),
        lax.psum_scatter(up_portion, "row", scatter_dimension=0, tiled=True),
        lax.psum_scatter(hidden_portion, "row", scatter_dimension=0, tiled=True),
    )
    hidden_state, gate_gradient, up_gradient = gated_back(gate_pre, up_pre, hid_grad)
    hidden_complete, gate_complete, up_complete = (
        lax.all_gather(hidden_state, "row", axis=0, tiled=True),
        lax.all_gather(gate_gradient, "row", axis=0, tiled=True),
        lax.all_gather(up_gradient, "row", axis=0, tiled=True),
    )
    gate_cotangent = product_transposed(gate_complete, gate_adapter_second)
    up_cotangent = product_transposed(up_complete, up_adapter_second)
    hidden_cotangent = matrix_product(hidden_complete, down_adapter_first)
    sum_bgate, sum_bup, sum_bhidden = lax.psum(
        (gate_cotangent, up_cotangent, hidden_cotangent), "col"
    )
    gate_low, up_low, hidden_reduced = (
        lax.all_gather(sum_bgate.astype(jnp.bfloat16), "row", axis=1, tiled=True),
        lax.all_gather(sum_bup.astype(jnp.bfloat16), "row", axis=1, tiled=True),
        lax.all_gather(sum_bhidden.astype(jnp.bfloat16), "row", axis=1, tiled=True),
    )
    col_start = col_index * rank_column
    gate_reduced_column = lax.dynamic_slice_in_dim(gate_low, col_start, rank_column, 1)
    up_reduced_column = lax.dynamic_slice_in_dim(up_low, col_start, rank_column, 1)
    hidden_low_col = lax.dynamic_slice_in_dim(hidden_reduced, col_start, rank_column, 1)
    input_portion = product_transposed(gate_complete, gate_matrix) + product_transposed(
        up_complete, up_matrix
    )
    input_portion = (
        input_portion
        + product_transposed(gate_reduced_column, gate_adapter_first)
        + product_transposed(up_reduced_column, up_adapter_first)
    )
    input_grad = lax.psum_scatter(input_portion, "col", scatter_dimension=0, tiled=True).astype(
        jnp.bfloat16
    )
    grad_gate_in = product_tn(input_row_block, gate_reduced_column)
    grad_gate_out = product_tn(reduced_gate_row, gate_complete)
    grad_up_in = product_tn(input_row_block, up_reduced_column)
    grad_up_out = product_tn(reduced_up_row, up_complete)
    grad_down_in = product_tn(hidden_complete, reduced_cotangent_row)
    grad_down_out = product_tn(hidden_low_col, cotangent_rows)
    return (
        input_grad,
        grad_gate_in,
        grad_gate_out,
        grad_up_in,
        grad_up_out,
        grad_down_in,
        grad_down_out,
    )


def solution(mesh):
    return jax.shard_map(
        on_device,
        mesh=mesh,
        in_specs=(
            P("col", "row"),
            P("col", "row"),
            P("row", "col"),
            P("row", "col"),
            P("col", "row"),
            P("row", "col"),
            P("row", "col"),
            P("row", "col"),
            P("row", "col"),
            P("col", "row"),
            P("col", "row"),
        ),
        out_specs=(
            P("col", "row"),
            P("row", "col"),
            P("row", "col"),
            P("row", "col"),
            P("row", "col"),
            P("col", "row"),
            P("col", "row"),
        ),
        check_vma=False,
    )
```

profile of v0, /device:TPU:2, one launch (start us, length us, event | category | flops | bytes accessed | tf_op | source)
XLA Modules:
  0.0 705.9 jit_solution(5695515283411741139)
XLA Ops:
  7.2 0.7 all-gather.6.cloned.1.call-update
  8.0 0.7 all-gather.8.cloned.1.call-update
  8.7 51.8 %all-gather.6.cloned.1.call-done = bf16[512,1024]{1,0:T(8,128)(2,1)} async-done(((bf16[32,1024]{1,0:T(8,128)(2,1)}), bf16[512,1024]{1,0:T(8,128)(2,1)}) %all-gather.6.cloned.1.call-update) | async-done | bytes 1048592 | tf_op jit(solution)/shard_map/all_gather | solution.py:51
  60.6 1.6 fusion.29
  62.2 47.7 %all-gather.8.cloned.1.call-done = bf16[512,1024]{1,0:T(8,128)(2,1)} async-done(((bf16[32,1024]{1,0:T(8,128)(2,1)}), bf16[512,1024]{1,0:T(8,128)(2,1)}) %all-gather.8.cloned.1.call-update) | async-done | bytes 1048592 | tf_op jit(solution)/shard_map/all_gather | solution.py:50
  109.9 2.3 fusion.33
  112.2 2.3 fusion.31
  114.5 48.4 %all-reduce.4 = (bf16[512,32]{0,1:T(8,128)(2,1)}, bf16[512,32]{0,1:T(8,128)(2,1)S(1)}, bf16[512,32]{0,1:T(8,128)(2,1)}) all-reduce(f32[512,32]{0,1:T(8,128)} %fusion.33, f32[512,32]{0,1:T(8,128)S(1)} %fusion.29, f32[512,32]{0,1:T(8,128)} %fusion.31), channel_id=1, replica_groups=mesh['row'=16,'col'=16] {'row'}, use_global_device_ids=true, to_apply=%region_4.0 | all-reduce | flops 49152 | bytes 294912 | tf_op jit(solution)/shard_map/psum | solution.py:58
  162.8 22.4 %all_gather.34 = bf16[512,512]{0,1:T(8,128)(2,1)S(1)} all-gather(bf16[512,32]{0,1:T(8,128)(2,1)S(1)} %get-tuple-element.11), channel_id=1, replica_groups=mesh['row'=16,'col'=16] {'col'}, dimensions={1}, use_global_device_ids=true | all-gather | bytes 557056 | tf_op jit(solution)/shard_map/all_gather | solution.py:62
  185.3 4.6 fusion.28
  189.9 2.3 convolution_add_fusion.2
  192.3 0.7 copy-done.21
  193.0 22.6 %all_gather.37 = bf16[512,512]{0,1:T(8,128)(2,1)S(1)} all-gather(bf16[512,32]{0,1:T(8,128)(2,1)S(1)} %copy-done.21), channel_id=1, replica_groups=mesh['row'=16,'col'=16] {'col'}, dimensions={1}, use_global_device_ids=true | all-gather | bytes 557056 | tf_op jit(solution)/shard_map/all_gather | solution.py:60
  215.6 3.5 fusion.32
  219.1 2.4 convolution_add_fusion
  221.6 0.7 copy-done.19
  222.3 22.4 %all_gather.36 = bf16[512,512]{0,1:T(8,128)(2,1)S(1)} all-gather(bf16[512,32]{0,1:T(8,128)(2,1)S(1)} %copy-done.19), channel_id=1, replica_groups=mesh['row'=16,'col'=16] {'col'}, dimensions={1}, use_global_device_ids=true | all-gather | bytes 557056 | tf_op jit(solution)/shard_map/all_gather | solution.py:61
  244.7 4.6 fusion.30
  249.3 2.4 convolution_add_fusion.1
  251.8 2.9 reduce-scatter.5.cloned.1.call-done
  254.7 62.9 %reduce-scatter.9.cloned.1.call-done = f32[32,1664]{1,0:T(8,128)} async-done(((f32[512,1664]{1,0:T(8,128)}), f32[32,1664]{1,0:T(8,128)}) %reduce-scatter.9.cloned.1.call-update) | async-done | bytes 213008 | tf_op jit(solution)/shard_map/reduce_scatter | solution.py:80
  317.6 63.1 %reduce-scatter.7.cloned.1.call-done = f32[32,1664]{1,0:T(8,128)} async-done(((f32[512,1664]{1,0:T(8,128)}), f32[32,1664]{1,0:T(8,128)}) %reduce-scatter.7.cloned.1.call-update) | async-done | bytes 213008 | tf_op jit(solution)/shard_map/reduce_scatter | solution.py:81
  380.7 1.9 multiply_convert_fusion
  382.7 0.7 all-gather.12.cloned.1.call-update
  383.5 0.7 all-gather.10.cloned.1.call-update
  384.2 36.6 %all-gather.14.cloned.1.call-done = bf16[512,1664]{1,0:T(8,128)(2,1)} async-done(((bf16[32,1664]{1,0:T(8,128)(2,1)}), bf16[512,1664]{1,0:T(8,128)(2,1)}) %all-gather.14.cloned.1.call-update) | async-done | bytes 1703952 | tf_op jit(solution)/shard_map/all_gather | solution.py:86
  420.8 2.7 fusion.38
  423.5 37.5 %all-gather.12.cloned.1.call-done = bf16[512,1664]{1,0:T(8,128)(2,1)} async-done(((bf16[32,1664]{1,0:T(8,128)(2,1)}), bf16[512,1664]{1,0:T(8,128)(2,1)}) %all-gather.12.cloned.1.call-update) | async-done | bytes 1703952 | tf_op jit(solution)/shard_map/all_gather | solution.py:88
  461.0 2.7 fusion.37
  463.7 37.5 %all-gather.10.cloned.1.call-done = bf16[512,1664]{1,0:T(8,128)(2,1)} async-done(((bf16[32,1664]{1,0:T(8,128)(2,1)}), bf16[512,1664]{1,0:T(8,128)(2,1)}) %all-gather.10.cloned.1.call-update) | async-done | bytes 1703952 | tf_op jit(solution)/shard_map/all_gather | solution.py:87
  501.2 2.7 fusion.36
  503.9 72.1 %all-reduce.5 = (bf16[512,32]{0,1:T(8,128)(2,1)}, bf16[512,32]{0,1:T(8,128)(2,1)}, bf16[512,32]{0,1:T(8,128)(2,1)}) all-reduce(f32[512,32]{0,1:T(8,128)} %fusion.36, f32[512,32]{0,1:T(8,128)} %fusion.37, f32[512,32]{0,1:T(8,128)S(1)} %copy-done.18), channel_id=1, replica_groups=mesh['row'=16,'col'=16] {'col'}, use_global_device_ids=true, to_apply=%region_6.0 | all-reduce | flops 49152 | bytes 294912 | tf_op jit(solution)/shard_map/psum | solution.py:93
  576.1 17.3 %all_gather.40 = bf16[512,512]{0,1:T(8,128)(2,1)S(1)} all-gather(bf16[512,32]{0,1:T(8,128)(2,1)} %get-tuple-element.7), channel_id=1, replica_groups=mesh['row'=16,'col'=16] {'row'}, dimensions={1}, use_global_device_ids=true | all-gather | bytes 557056 | tf_op jit(solution)/shard_map/all_gather | solution.py:97
  593.4 16.5 %all_gather.41 = bf16[512,512]{0,1:T(8,128)(2,1)S(1)} all-gather(bf16[512,32]{0,1:T(8,128)(2,1)} %get-tuple-element.8), channel_id=1, replica_groups=mesh['row'=16,'col'=16] {'row'}, dimensions={1}, use_global_device_ids=true | all-gather | bytes 557056 | tf_op jit(solution)/shard_map/all_gather | solution.py:98
  610.0 0.5 fusion.6
  610.5 2.1 fusion.34
  612.9 2.1 fusion.35
  615.0 1.8 add_add_fusion
  616.9 0.7 copy-done.20
  617.6 17.8 %all_gather.43 = bf16[512,512]{0,1:T(8,128)(2,1)S(1)} all-gather(bf16[512,32]{0,1:T(8,128)(2,1)S(1)} %copy-done.20), channel_id=1, replica_groups=mesh['row'=16,'col'=16] {'row'}, dimensions={1}, use_global_device_ids=true | all-gather | bytes 557056 | tf_op jit(solution)/shard_map/all_gather | solution.py:99
  635.4 2.2 convolution_bitcast_fusion.1
  637.6 2.3 convolution_bitcast_fusion
  640.0 0.9 fusion.1
  640.9 2.0 fusion.14
  642.9 1.9 fusion.8
  644.8 1.9 fusion.11
  646.6 51.2 %reduce-scatter.11.cloned.1.call-done = f32[32,1024]{1,0:T(8,128)} async-done(((f32[512,1024]{1,0:T(8,128)}), f32[32,1024]{1,0:T(8,128)}) %reduce-scatter.11.cloned.1.call-update) | async-done | bytes 131088 | tf_op jit(solution)/shard_map/reduce_scatter | solution.py:113
  697.8 1.5 convert_element_type.37
  (57 shorter events, 0.9 us)
Async XLA Ops:
  7.2 208.4 %copy-start = (bf16[1024,1664]{1,0:T(8,128)(2,1)S(1)}, bf16[1024,1664]{1,0:T(8,128)(2,1)}, u32[]{:S(2)}) copy-start(bf16[1024,1664]{1,0:T(8,128)(2,1)} %param.13) | copy-start | bytes 10223620
  7.2 105.0 %copy-start.15 = (bf16[1024,32]{0,1:T(8,128)(2,1)S(1)}, bf16[1024,32]{0,1:T(8,128)(2,1)}, u32[]{:S(2)}) copy-start(bf16[1024,32]{0,1:T(8,128)(2,1)} %param.18) | copy-start | bytes 196612
  7.2 53.4 %all-gather.6.cloned.1.call-start = ((), (), s32[]{:S(2)}) async-start(), calls=%async_computation.4 | async-start | bytes 1114112 | tf_op jit(solution)/shard_map/all_gather | solution.py:51
  7.9 102.0 %all-gather.8.cloned.1.call-start = ((), (), s32[]{:S(2)}) async-start(), calls=%async_computation.6 | async-start | bytes 1114112 | tf_op jit(solution)/shard_map/all_gather | solution.py:50
  8.7 246.0 %reduce-scatter.5.cloned.1.call-start = ((), (), s32[]{:S(2)}) async-start(), calls=%async_computation.5 | async-start | bytes 3620864 | tf_op jit(solution)/shard_map/reduce_scatter | solution.py:82
  185.3 4.6 copy-start.7
  185.3 4.6 copy-start.12
  192.2 0.8 copy-start.21
  192.3 125.3 %reduce-scatter.9.cloned.1.call-start = ((), (), s32[]{:S(2)}) async-start(), calls=%async_computation.8 | async-start | bytes 3620864 | tf_op jit(solution)/shard_map/reduce_scatter | solution.py:80
  215.6 3.5 copy-start.8
  215.6 3.5 copy-start.14
  221.5 0.8 copy-start.19
  221.5 159.1 %reduce-scatter.7.cloned.1.call-start = ((), (), s32[]{:S(2)}) async-start(), calls=%async_computation.7 | async-start | bytes 3620864 | tf_op jit(solution)/shard_map/reduce_scatter | solution.py:81
  244.7 4.6 copy-start.9
  244.7 4.6 copy-start.13
  251.8 169.0 %all-gather.14.cloned.1.call-start = ((), (), s32[]{:S(2)}) async-start(), calls=%async_computation.12 | async-start | bytes 1810432 | tf_op jit(solution)/shard_map/all_gather | solution.py:86
  382.7 78.4 %all-gather.12.cloned.1.call-start = ((), (), s32[]{:S(2)}) async-start(), calls=%async_computation.10 | async-start | bytes 1810432 | tf_op jit(solution)/shard_map/all_gather | solution.py:88
  383.4 117.8 %all-gather.10.cloned.1.call-start = ((), (), s32[]{:S(2)}) async-start(), calls=%async_computation.9 | async-start | bytes 1810432 | tf_op jit(solution)/shard_map/all_gather | solution.py:87
  384.2 313.7 %reduce-scatter.11.cloned.1.call-start = ((), (), s32[]{:S(2)}) async-start(), calls=%async_computation.11 | async-start | bytes 2228224 | tf_op jit(solution)/shard_map/reduce_scatter | solution.py:113
  423.5 80.4 %copy-start.18 = (f32[512,32]{0,1:T(8,128)S(1)}, f32[512,32]{0,1:T(8,128)}, u32[]{:S(2)}) copy-start(f32[512,32]{0,1:T(8,128)} %fusion.38) | copy-start | bytes 196612
  423.5 186.5 %copy-start.17 = (bf16[1024,32]{0,1:T(8,128)(2,1)S(1)}, bf16[1024,32]{0,1:T(8,128)(2,1)}, u32[]{:S(2)}) copy-start(bf16[1024,32]{0,1:T(8,128)(2,1)} %param.16) | copy-start | bytes 196612
  576.1 34.3 %copy-start.4 = (bf16[512,1664]{1,0:T(8,128)(2,1)S(1)}, bf16[512,1664]{1,0:T(8,128)(2,1)}, u32[]{:S(2)}) copy-start(bf16[512,1664]{1,0:T(8,128)(2,1)} %all-gather.10.cloned.1.call-done) | copy-start | bytes 5111812
  593.4 16.5 %copy-start.11 = (bf16[512,512]{0,1:T(8,128)(2,1)}, bf16[512,512]{0,1:T(8,128)(2,1)S(1)}, u32[]{:S(2)}) copy-start(bf16[512,512]{0,1:T(8,128)(2,1)S(1)} %all_gather.40) | copy-start | bytes 1572868
  610.0 5.0 copy-start.10
  610.4 2.1 copy-start.2
  610.4 2.5 copy-start.22
  612.9 2.1 copy-start.16
  616.8 0.8 copy-start.20
  616.9 23.1 %copy-start.6 = (bf16[512,1024]{1,0:T(8,128)(2,1)S(1)}, bf16[512,1024]{1,0:T(8,128)(2,1)}, u32[]{:S(2)}) copy-start(bf16[512,1024]{1,0:T(8,128)(2,1)} %all-gather.6.cloned.1.call-done) | copy-start | bytes 3145732
  617.6 23.3 %copy-start.1 = (bf16[512,1664]{1,0:T(8,128)(2,1)S(1)}, bf16[512,1664]{1,0:T(8,128)(2,1)}, u32[]{:S(2)}) copy-start(bf16[512,1664]{1,0:T(8,128)(2,1)} %all-gather.14.cloned.1.call-done) | copy-start | bytes 5111812
  637.6 5.3 copy-start.5
  640.9 3.8 copy-start.3
Sparse Core Ops, SparseCore 0:
  10.4 50.0 all-gather.5
  63.0 46.8 all-gather.7
  192.4 62.2 reduce-scatter.4
  257.1 60.4 reduce-scatter.8
  320.0 60.6 reduce-scatter.6
  382.9 37.8 all-gather.13
  423.2 37.7 all-gather.11
  463.4 37.7 all-gather.9
  617.0 80.7 reduce-scatter.10
where the time goes:
time: 707 us; the launch traced here: 706 us
  waiting for transfers between devices  394 us (56%)
  blocking collectives  240 us (34%)
  matrix products  51.7 us (7%)
  between operations  14.1 us (2%)
    psum x1, blocking collectives, on_device(): lax.psum((gate_cotangent, up_cotangent, hidden_cotangent), 'col')  72.1 us
    reduce_scatter x1, waiting for transfers between devices, on_device(): lax.psum_scatter(up_portion, 'row', scatter_dimension=0, tiled=True)  63.1 us
    reduce_scatter x1, waiting for transfers between devices, on_device(): lax.psum_scatter(gate_portion, 'row', scatter_dimension=0, tiled=True)  62.9 us
    all_gather x1, waiting for transfers between devices, on_device(): lax.all_gather(output_gradient, 'col', axis=0, tiled=True)  51.8 us
    reduce_scatter x1, waiting for transfers between devices, on_device(): lax.psum_scatter(input_portion, 'col', scatter_dimension=0, tiled=True)  51.2 us
    psum x1, blocking collectives, on_device(): lax.psum((portion_gate, portion_up, portion_down), 'row')  48.4 us
    all_gather x1, waiting for transfers between devices, on_device(): lax.all_gather(inputs, 'col', axis=0, tiled=True)  47.7 us
    all_gather x1, waiting for transfers between devices, on_device(): lax.all_gather(gate_gradient, 'row', axis=0, tiled=True)  37.5 us
  transfers between devices with their start and end apart: 9, of which 9 were waited for; matrix products, arithmetic and copies ran while one was open for 4% of the time, Pallas kernels for 0%

commit v1 on v0

--- a/solution.py
+++ b/solution.py
@@ -85,7 +85,9 @@
     hidden_complete, gate_complete, up_complete = (
         lax.all_gather(hidden_state, "row", axis=0, tiled=True),
         lax.all_gather(gate_gradient, "row", axis=0, tiled=True),
-        lax.all_gather(up_gradient, "row", axis=0, tiled=True),
+        jnp.concatenate(
+            lax.all_to_all(jnp.stack([up_gradient] * lax.axis_size("row")), "row", 0, 0), axis=0
+        ),
     )
     gate_cotangent = product_transposed(gate_complete, gate_adapter_second)
     up_cotangent = product_transposed(up_complete, up_adapter_second)

time: 707 us -> 685 us (0.969)
  waiting for transfers between devices: 394 us -> 362 us
    all_gather x1 -> x0, waiting for transfers between devices: 37.5 us -> none  [on_device(): lax.all_gather(up_gradient, 'row', axis=0, tiled=True)]
    all_gather x1, waiting for transfers between devices: 36.6 us -> 46.4 us  [on_device(): lax.all_gather(hidden_state, 'row', axis=0, tiled=True)]
  transfers between devices with their start and end apart: 9 -> 9, of which waited for: 9 -> 8; matrix products, arithmetic and copies ran while one was open for 4% -> 6% of each run, Pallas kernels for 0% -> 0%
where the time goes in v1:
time: 685 us; the launch traced here: 684 us
  waiting for transfers between devices  362 us (53%)
  blocking collectives  239 us (35%)
  matrix products  58.3 us (9%)
  between operations  14.4 us (2%)
    psum x1, blocking collectives, on_device(): lax.psum((gate_cotangent, up_cotangent, hidden_cotangent), 'col')  71.6 us
    reduce_scatter x1, waiting for transfers between devices, on_device(): lax.psum_scatter(up_portion, 'row', scatter_dimension=0, tiled=True)  63.1 us
    reduce_scatter x1, waiting for transfers between devices, on_device(): lax.psum_scatter(gate_portion, 'row', scatter_dimension=0, tiled=True)  63 us
    all_gather x1, waiting for transfers between devices, on_device(): lax.all_gather(output_gradient, 'col', axis=0, tiled=True)  51.8 us
    reduce_scatter x1, waiting for transfers between devices, on_device(): lax.psum_scatter(input_portion, 'col', scatter_dimension=0, tiled=True)  51.2 us
    psum x1, blocking collectives, on_device(): lax.psum((portion_gate, portion_up, portion_down), 'row')  48.9 us
    all_gather x1, waiting for transfers between devices, on_device(): lax.all_gather(inputs, 'col', axis=0, tiled=True)  47.7 us
    all_gather x1, waiting for transfers between devices, on_device(): lax.all_gather(hidden_state, 'row', axis=0, tiled=True)  46.4 us
  transfers between devices with their start and end apart: 9, of which 8 were waited for; matrix products, arithmetic and copies ran while one was open for 6% of the time, Pallas kernels for 0%

profile of v1, /device:TPU:2, one launch (start us, length us, event | category | flops | bytes accessed | tf_op | source)
XLA Modules:
  0.0 683.5 jit_solution(13827126708538852089)
XLA Ops:
  7.2 0.7 all-gather.5.cloned.1.call-update
  8.0 0.7 all-gather.7.cloned.1.call-update
  8.7 51.8 %all-gather.5.cloned.1.call-done = bf16[512,1024]{1,0:T(8,128)(2,1)} async-done(((bf16[32,1024]{1,0:T(8,128)(2,1)}), bf16[512,1024]{1,0:T(8,128)(2,1)}) %all-gather.5.cloned.1.call-update) | async-done | bytes 1048592 | tf_op jit(solution)/shard_map/all_gather | solution.py:51
  60.6 1.6 fusion.29
  62.2 47.7 %all-gather.7.cloned.1.call-done = bf16[512,1024]{1,0:T(8,128)(2,1)} async-done(((bf16[32,1024]{1,0:T(8,128)(2,1)}), bf16[512,1024]{1,0:T(8,128)(2,1)}) %all-gather.7.cloned.1.call-update) | async-done | bytes 1048592 | tf_op jit(solution)/shard_map/all_gather | solution.py:50
  109.9 2.3 fusion.33
  112.2 2.3 fusion.31
  114.5 48.9 %all-reduce.4 = (bf16[512,32]{0,1:T(8,128)(2,1)S(1)}, bf16[512,32]{0,1:T(8,128)(2,1)}, bf16[512,32]{0,1:T(8,128)(2,1)S(1)}) all-reduce(f32[512,32]{0,1:T(8,128)} %fusion.33, f32[512,32]{0,1:T(8,128)S(1)} %fusion.29, f32[512,32]{0,1:T(8,128)} %fusion.31), channel_id=1, replica_groups=mesh['row'=16,'col'=16] {'row'}, use_global_device_ids=true, to_apply=%region_4.0 | all-reduce | flops 49152 | bytes 294912 | tf_op jit(solution)/shard_map/psum | solution.py:58
  163.4 22.5 %all_gather.31 = bf16[512,512]{0,1:T(8,128)(2,1)S(1)} all-gather(bf16[512,32]{0,1:T(8,128)(2,1)} %get-tuple-element.11), channel_id=1, replica_groups=mesh['row'=16,'col'=16] {'col'}, dimensions={1}, use_global_device_ids=true | all-gather | bytes 557056 | tf_op jit(solution)/shard_map/all_gather | solution.py:62
  185.9 4.6 fusion.28
  190.5 2.4 convolution_add_fusion.2
  192.9 0.0 reduce-scatter.9.cloned.1.call-start
  193.0 22.6 %all_gather.34 = bf16[512,512]{0,1:T(8,128)(2,1)S(1)} all-gather(bf16[512,32]{0,1:T(8,128)(2,1)S(1)} %get-tuple-element.10), channel_id=1, replica_groups=mesh['row'=16,'col'=16] {'col'}, dimensions={1}, use_global_device_ids=true | all-gather | bytes 557056 | tf_op jit(solution)/shard_map/all_gather | solution.py:60
  215.6 4.6 fusion.32
  220.2 2.4 convolution_add_fusion
  222.6 0.0 reduce-scatter.7.cloned.1.call-start
  222.6 22.4 %all_gather.33 = bf16[512,512]{0,1:T(8,128)(2,1)S(1)} all-gather(bf16[512,32]{0,1:T(8,128)(2,1)S(1)} %get-tuple-element.12), channel_id=1, replica_groups=mesh['row'=16,'col'=16] {'col'}, dimensions={1}, use_global_device_ids=true | all-gather | bytes 557056 | tf_op jit(solution)/shard_map/all_gather | solution.py:61
  245.1 3.5 fusion.30
  248.6 2.4 convolution_add_fusion.1
  251.1 2.9 reduce-scatter.5.cloned.1.call-done
  254.1 63.0 %reduce-scatter.9.cloned.1.call-done = f32[32,1664]{1,0:T(8,128)} async-done(((f32[512,1664]{1,0:T(8,128)}), f32[32,1664]{1,0:T(8,128)}) %reduce-scatter.9.cloned.1.call-update) | async-done | bytes 213008 | tf_op jit(solution)/shard_map/reduce_scatter | solution.py:80
  317.1 63.1 %reduce-scatter.7.cloned.1.call-done = f32[32,1664]{1,0:T(8,128)} async-done(((f32[512,1664]{1,0:T(8,128)}), f32[32,1664]{1,0:T(8,128)}) %reduce-scatter.7.cloned.1.call-update) | async-done | bytes 213008 | tf_op jit(solution)/shard_map/reduce_scatter | solution.py:81
  380.1 1.9 multiply_convert_fusion
  382.1 1.3 stack.2
  383.4 4.7 all-to-all-start
  388.2 0.7 all-gather.9.cloned.1.call-update
  388.9 0.2 reduce-scatter.11.cloned.1.call-start
  389.1 46.4 %all-gather.11.cloned.1.call-done = bf16[512,1664]{1,0:T(8,128)(2,1)} async-done(((bf16[32,1664]{1,0:T(8,128)(2,1)}), bf16[512,1664]{1,0:T(8,128)(2,1)}) %all-gather.11.cloned.1.call-update) | async-done | bytes 1703952 | tf_op jit(solution)/shard_map/all_gather | solution.py:86
  435.5 2.7 fusion.38
  438.2 2.7 fusion.37
  440.9 4.9 fusion.35
  445.8 33.4 %all-gather.9.cloned.1.call-done = bf16[512,1664]{1,0:T(8,128)(2,1)} async-done(((bf16[32,1664]{1,0:T(8,128)(2,1)}), bf16[512,1664]{1,0:T(8,128)(2,1)}) %all-gather.9.cloned.1.call-update) | async-done | bytes 1703952 | tf_op jit(solution)/shard_map/all_gather | solution.py:87
  479.2 2.7 fusion.36
  481.9 71.6 %all-reduce.5 = (bf16[512,32]{0,1:T(8,128)(2,1)S(1)}, bf16[512,32]{0,1:T(8,128)(2,1)S(1)}, bf16[512,32]{0,1:T(8,128)(2,1)S(1)}) all-reduce(f32[512,32]{0,1:T(8,128)} %fusion.36, f32[512,32]{0,1:T(8,128)} %fusion.37, f32[512,32]{0,1:T(8,128)} %fusion.38), channel_id=1, replica_groups=mesh['row'=16,'col'=16] {'col'}, use_global_device_ids=true, to_apply=%region_6.0 | all-reduce | flops 49152 | bytes 294912 | tf_op jit(solution)/shard_map/psum | solution.py:95
  553.5 17.1 %all_gather.36 = bf16[512,512]{0,1:T(8,128)(2,1)S(1)} all-gather(bf16[512,32]{0,1:T(8,128)(2,1)S(1)} %get-tuple-element.7), channel_id=1, replica_groups=mesh['row'=16,'col'=16] {'row'}, dimensions={1}, use_global_device_ids=true | all-gather | bytes 557056 | tf_op jit(solution)/shard_map/all_gather | solution.py:99
  570.6 16.1 %all_gather.37 = bf16[512,512]{0,1:T(8,128)(2,1)S(1)} all-gather(bf16[512,32]{0,1:T(8,128)(2,1)S(1)} %get-tuple-element.8), channel_id=1, replica_groups=mesh['row'=16,'col'=16] {'row'}, dimensions={1}, use_global_device_ids=true | all-gather | bytes 557056 | tf_op jit(solution)/shard_map/all_gather | solution.py:100
  586.7 1.3 fusion.6
  588.1 4.2 fusion.34
  592.4 1.8 add_add_fusion
  594.2 17.9 %all_gather.39 = bf16[512,512]{0,1:T(8,128)(2,1)S(1)} all-gather(bf16[512,32]{0,1:T(8,128)(2,1)S(1)} %get-tuple-element.9), channel_id=1, replica_groups=mesh['row'=16,'col'=16] {'row'}, dimensions={1}, use_global_device_ids=true | all-gather | bytes 557056 | tf_op jit(solution)/shard_map/all_gather | solution.py:101
  612.1 2.2 convolution_bitcast_fusion.1
  614.3 2.3 convolution_bitcast_fusion
  616.6 0.9 fusion.1
  617.5 2.7 fusion.11
  620.3 1.9 fusion.14
  622.1 1.9 fusion.8
  624.0 51.2 %reduce-scatter.11.cloned.1.call-done = f32[32,1024]{1,0:T(8,128)} async-done(((f32[512,1024]{1,0:T(8,128)}), f32[32,1024]{1,0:T(8,128)}) %reduce-scatter.11.cloned.1.call-update) | async-done | bytes 131088 | tf_op jit(solution)/shard_map/reduce_scatter | solution.py:115
  675.1 1.5 convert_element_type.37
  (47 shorter events, 0.4 us)
Async XLA Ops:
  7.2 237.9 %copy-start = (bf16[1024,1664]{1,0:T(8,128)(2,1)S(1)}, bf16[1024,1664]{1,0:T(8,128)(2,1)}, u32[]{:S(2)}) copy-start(bf16[1024,1664]{1,0:T(8,128)(2,1)} %param.14) | copy-start | bytes 10223620
  7.2 105.0 %copy-start.16 = (bf16[1024,32]{0,1:T(8,128)(2,1)S(1)}, bf16[1024,32]{0,1:T(8,128)(2,1)}, u32[]{:S(2)}) copy-start(bf16[1024,32]{0,1:T(8,128)(2,1)} %param.18) | copy-start | bytes 196612
  7.2 53.4 %all-gather.5.cloned.1.call-start = ((), (), s32[]{:S(2)}) async-start(), calls=%async_computation.5 | async-start | bytes 1114112 | tf_op jit(solution)/shard_map/all_gather | solution.py:51
  7.9 102.0 %all-gather.7.cloned.1.call-start = ((), (), s32[]{:S(2)}) async-start(), calls=%async_computation.7 | async-start | bytes 1114112 | tf_op jit(solution)/shard_map/all_gather | solution.py:50
  8.7 245.4 %reduce-scatter.5.cloned.1.call-start = ((), (), s32[]{:S(2)}) async-start(), calls=%async_computation.6 | async-start | bytes 3620864 | tf_op jit(solution)/shard_map/reduce_scatter | solution.py:82
  185.9 4.6 copy-start.6
  185.9 4.6 copy-start.11
  192.9 124.1 %reduce-scatter.9.cloned.1.call-start = ((), (), s32[]{:S(2)}) async-start(), calls=%async_computation.9 | async-start | bytes 3620864 | tf_op jit(solution)/shard_map/reduce_scatter | solution.py:80
  215.5 4.6 copy-start.7
  215.5 4.6 copy-start.14
  222.6 157.5 %reduce-scatter.7.cloned.1.call-start = ((), (), s32[]{:S(2)}) async-start(), calls=%async_computation.8 | async-start | bytes 3620864 | tf_op jit(solution)/shard_map/reduce_scatter | solution.py:81
  245.1 3.5 copy-start.8
  245.1 3.5 copy-start.13
  251.1 184.4 %all-gather.11.cloned.1.call-start = ((), (), s32[]{:S(2)}) async-start(), calls=%async_computation.12 | async-start | bytes 1810432 | tf_op jit(solution)/shard_map/all_gather | solution.py:86
  383.4 52.1 %copy-start.12 = (bf16[1664,32]{0,1:T(8,128)(2,1)S(1)}, bf16[1664,32]{0,1:T(8,128)(2,1)}, u32[]{:S(2)}) copy-start(bf16[1664,32]{0,1:T(8,128)(2,1)} %param.20) | copy-start | bytes 319492
  383.4 54.8 %all-to-all-start = ((bf16[16,32,1664]{2,1,0:T(8,128)(2,1)}), bf16[16,32,1664]{2,1,0:T(8,128)(2,1)}, u32[]{:S(2)}, u32[]{:S(2)}) async-start(bf16[16,32,1664]{2,1,0:T(8,128)(2,1)} %stack.2), calls=%async_computation.3 | async-start | bytes 3407872 | tf_op jit(solution)/shard_map/all_to_all | solution.py:89
  388.1 91.1 %all-gather.9.cloned.1.call-start = ((), (), s32[]{:S(2)}) async-start(), calls=%async_computation.10 | async-start | bytes 1810432 | tf_op jit(solution)/shard_map/all_gather | solution.py:87
  388.9 286.2 %reduce-scatter.11.cloned.1.call-start = ((), (), s32[]{:S(2)}) async-start(), calls=%async_computation.11 | async-start | bytes 2228224 | tf_op jit(solution)/shard_map/reduce_scatter | solution.py:115
  440.9 38.3 %copy-start.15 = (bf16[32,1664]{1,0:T(8,128)(2,1)S(1)}, bf16[32,1664]{1,0:T(8,128)(2,1)}, u32[]{:S(2)}) copy-start(bf16[32,1664]{1,0:T(8,128)(2,1)} %param.17) | copy-start | bytes 319492
  553.5 34.6 %copy-start.2 = (bf16[512,1664]{1,0:T(8,128)(2,1)S(1)}, bf16[512,1664]{1,0:T(8,128)(2,1)}, u32[]{:S(2)}) copy-start(bf16[512,1664]{1,0:T(8,128)(2,1)} %all-gather.9.cloned.1.call-done) | copy-start | bytes 5111812
  570.6 16.1 %copy-start.10 = (bf16[512,512]{0,1:T(8,128)(2,1)}, bf16[512,512]{0,1:T(8,128)(2,1)S(1)}, u32[]{:S(2)}) copy-start(bf16[512,512]{0,1:T(8,128)(2,1)S(1)} %all_gather.36) | copy-start | bytes 1572868
  586.7 5.6 copy-start.9
  588.1 4.3 copy-start.5
  588.1 4.3 copy-start.17
  594.2 22.4 %copy-start.4 = (bf16[512,1024]{1,0:T(8,128)(2,1)S(1)}, bf16[512,1024]{1,0:T(8,128)(2,1)}, u32[]{:S(2)}) copy-start(bf16[512,1024]{1,0:T(8,128)(2,1)} %all-gather.5.cloned.1.call-done) | copy-start | bytes 3145732
  614.3 6.0 copy-start.1
  617.5 4.6 copy-start.3
Sparse Core Ops, SparseCore 0:
  10.4 50.0 all-gather.4
  63.0 46.8 all-gather.6
  193.0 60.9 reduce-scatter.4
  256.5 60.5 reduce-scatter.8
  319.5 60.6 reduce-scatter.6
  382.4 53.0 all-gather.10
  437.9 41.2 all-gather.8
  594.3 80.7 reduce-scatter.10
